TPU v7x, 32 devices: a whole 2x2x4 slice. The times are simulated.
32 devices in a mesh: groups: 2 (over y), ctx: 4 (over z), segment: 2 (over x), head: 2 (over core).
Axes of the slice: x: 2, y: 2, z: 4, core: 2. Of those that a mesh axis runs over, the one named last changes fastest.
Arguments:
- queries: bfloat16 [4, 2048, 4096], P(('groups', 'segment'), 'ctx', 'head'), parts along dimension 0, may hold values from -16 to 16
- span_key_values: bfloat16 [4, 2048, 2, 1024], P(('groups', 'segment'), 'ctx', None, 'head'), parts along dimension 0, may hold values from -6 to 6
- key_value_cache: bfloat16 [4, 16384, 2, 1024], P(('groups', 'segment'), 'ctx', None, 'head'), parts along dimension 0, may hold values from -12 to 12
- chosen: int32 [4, 4, 8, 8], P(('groups', 'segment'), None, 'head'), parts along dimension 0, may hold values from 0 to 31, as said below
- offset: int32 [4], P(('groups', 'segment')), parts along dimension 0, may hold values from 8192 to 16384, as said below
Outputs:
- handed: bfloat16 [4, 2048, 4096], P(('groups', 'segment'), 'ctx', 'head'), parts along dimension 0
There are 2 independent parts, one for each index of `groups`. A program takes and returns all parts, laid end to end along the dimension named above; each array names one. Nothing has to cross between parts.
Inputs may be any that keep to these rules, and one draw needn't show every extreme that they name: `offset`: the first section's span starts at 16384; every other section's at 512 times a whole number from 16 to 32. `chosen`: for a section whose span starts at o, each query block and KV head names 8 different cache blocks below o / 512, among them block 0 and block o / 512 - 1.
All inputs are finite; a program needn't handle non-finite values.
Results may differ from a plain program's by a relative error of at most 0.0085.
Values may be sent and summed in bfloat16 or wider, within the bound.
A program may use at most 128 MiB of HBM per device.

v0:
```python
import jax
import jax.numpy as jnp
from jax import lax
from jax.sharding import PartitionSpec as P

HEAD_SIZE = 128
BLOCK_TOKENS = 512
CHOSEN_BLOCKS = 8


ROPE_BASE = 500000.0


def swapped(x, axis, stride):
    return lax.ppermute(x, axis, [(i, i ^ 1 << stride) for i in range(lax.axis_size(axis))])


def passed_along(block, axis, distance):
    devices = range(lax.axis_size(axis))
    route = [((i - distance) % len(devices), i) for i in devices]
    return lax.ppermute(block, axis, route)


def apply_rotary(values, token_positions):
    half_dim = values.shape[-1] // 2
    frequencies = ROPE_BASE ** (-(2.0 * jnp.arange(half_dim, dtype=jnp.float32)) / values.shape[-1])
    angles = token_positions[:, None] * frequencies[None, :]
    cosine = jnp.cos(angles)[:, None, :]
    sine_part = jnp.sin(angles)[:, None, :]
    widened = values.astype(jnp.float32)
    first_half = widened[..., :half_dim]
    second_half = widened[..., half_dim:]
    joined = jnp.concatenate(
        [
            first_half * cosine - second_half * sine_part,
            second_half * cosine + first_half * sine_part,
        ],
        axis=-1,
    )
    return joined.astype(jnp.bfloat16)


def combine(earlier, later):
    maxima = jnp.maximum(earlier[0], later[0])
    first_factor = jnp.exp(earlier[0] - maxima)
    second_factor = jnp.exp(later[0] - maxima)
    totals = earlier[1] * first_factor + later[1] * second_factor
    weighted = earlier[2] * first_factor[..., None] + later[2] * second_factor[..., None]
    return (maxima, totals, weighted)


def local(queries, span_key_values, key_value_cache, chosen, offset):
    ctx_size = lax.axis_size("ctx")
    my_index = lax.axis_index("ctx")
    tok_rows = queries.shape[1]
    kv_heads = key_value_cache.shape[3] // HEAD_SIZE
    q_heads = queries.shape[2] // HEAD_SIZE
    per_value_head = q_heads // kv_heads
    members = ctx_size // kv_heads
    blocks_here = key_value_cache.shape[1] // BLOCK_TOKENS
    blocks_total = blocks_here * ctx_size
    q_blocks = chosen.shape[1]
    per_block = BLOCK_TOKENS // tok_rows
    key_rows = BLOCK_TOKENS // members
    own_rows = tok_rows // members
    my_head = my_index // members
    my_rank = my_index % members
    score_scale = HEAD_SIZE ** (-0.5)
    token_start = offset[0] + my_index * tok_rows
    token_positions = (token_start + jnp.arange(tok_rows, dtype=jnp.int32)).astype(jnp.float32)
    rot_query = apply_rotary(queries[0].reshape(tok_rows, q_heads, HEAD_SIZE), token_positions)
    rotated_key_rows = apply_rotary(
        span_key_values[0, :, 0].reshape(tok_rows, kv_heads, HEAD_SIZE), token_positions
    )
    fresh_values = span_key_values[0, :, 1].reshape(tok_rows, kv_heads, HEAD_SIZE)
    query_send = jnp.broadcast_to(
        rot_query.reshape(tok_rows, kv_heads, 1, per_value_head * HEAD_SIZE),
        (tok_rows, kv_heads, members, per_value_head * HEAD_SIZE),
    )
    query_send = query_send.reshape(tok_rows, ctx_size, per_value_head * HEAD_SIZE)
    pair_rows = jnp.concatenate([rotated_key_rows, fresh_values], axis=-1)
    pair_send = (
        pair_rows.reshape(members, own_rows, kv_heads, 2 * HEAD_SIZE)
        .transpose(1, 2, 0, 3)
        .reshape(own_rows, ctx_size, 2 * HEAD_SIZE)
    )
    query_recv, pair_recv = (
        lax.all_to_all(query_send, "ctx", split_axis=1, concat_axis=1, tiled=True),
        lax.all_to_all(pair_send, "ctx", split_axis=1, concat_axis=1, tiled=True),
    )
    picks_here = chosen[0]
    needed = jnp.any(
        picks_here[..., None] == jnp.arange(blocks_total, dtype=jnp.int32), axis=(0, 2)
    )
    needed_here = lax.dynamic_slice_in_dim(needed, my_index * blocks_here, blocks_here, axis=1)
    needed_here = needed_here.T.reshape(blocks_here, 1, kv_heads, 1, 1, 1)
    arranged_rows = (
        key_value_cache[0]
        .reshape(blocks_here, members, key_rows, 2, kv_heads, HEAD_SIZE)
        .transpose(0, 2, 4, 1, 3, 5)
    )
    arranged_rows = jnp.where(needed_here, arranged_rows, jnp.zeros((), jnp.bfloat16))
    tile_send = arranged_rows.reshape(blocks_here * key_rows, ctx_size, 2 * HEAD_SIZE)
    fetched = lax.all_to_all(tile_send, "ctx", split_axis=1, concat_axis=1, tiled=True)
    fetched = fetched.reshape(blocks_here, key_rows, ctx_size, 2 * HEAD_SIZE)
    maxima_parts = []
    totals_parts = []
    weighted_parts = []
    for index_of_block in range(q_blocks):
        block_ids = picks_here[index_of_block][my_head]
        owner_rank = block_ids // blocks_here
        slot_index = block_ids % blocks_here
        picked = fetched[slot_index, :, owner_rank]
        sel_keys = picked[..., :HEAD_SIZE].reshape(CHOSEN_BLOCKS * key_rows, HEAD_SIZE)
        sel_values = picked[..., HEAD_SIZE:].reshape(CHOSEN_BLOCKS * key_rows, HEAD_SIZE)
        first_source = index_of_block * per_block
        own_pairs = pair_recv[:, first_source : first_source + per_block]
        own_keys = own_pairs[..., :HEAD_SIZE].reshape(own_rows * per_block, HEAD_SIZE)
        own_values = own_pairs[..., HEAD_SIZE:].reshape(own_rows * per_block, HEAD_SIZE)
        query_rows = query_recv[:, first_source : first_source + per_block].reshape(
            tok_rows * per_block * per_value_head, HEAD_SIZE
        )
        sources = first_source + jnp.arange(per_block, dtype=jnp.int32)
        query_token = sources[None, :] * tok_rows + jnp.arange(tok_rows, dtype=jnp.int32)[:, None]
        query_token = jnp.broadcast_to(
            query_token[:, :, None], (tok_rows, per_block, per_value_head)
        ).reshape(-1)
        key_token = (
            sources[None, :] * tok_rows
            + my_rank * own_rows
            + jnp.arange(own_rows, dtype=jnp.int32)[:, None]
        )
        key_token = key_token.reshape(-1)
        sel_scores = (
            jnp.dot(query_rows, sel_keys.T, preferred_element_type=jnp.float32) * score_scale
        )
        own_scores = (
            jnp.dot(query_rows, own_keys.T, preferred_element_type=jnp.float32) * score_scale
        )
        causal = key_token[None, :] <= query_token[:, None]
        own_scores = jnp.where(causal, own_scores, -jnp.inf)
        maxima = jnp.maximum(jnp.max(sel_scores, axis=1), jnp.max(own_scores, axis=1))
        sel_weights = jnp.exp(sel_scores - maxima[:, None])
        own_weights = jnp.exp(own_scores - maxima[:, None])
        totals = jnp.sum(sel_weights, axis=1) + jnp.sum(own_weights, axis=1)
        weighted = jnp.dot(
            sel_weights, sel_values.astype(jnp.float32), precision=lax.Precision.HIGHEST
        )
        weighted = weighted + jnp.dot(
            own_weights, own_values.astype(jnp.float32), precision=lax.Precision.HIGHEST
        )
        maxima_parts.append(maxima.reshape(tok_rows, per_block, per_value_head))
        totals_parts.append(totals.reshape(tok_rows, per_block, per_value_head))
        weighted_parts.append(weighted.reshape(tok_rows, per_block, per_value_head, HEAD_SIZE))
    maxima_all = jnp.concatenate(maxima_parts, axis=1)
    totals_all = jnp.concatenate(totals_parts, axis=1)
    weighted_all = jnp.concatenate(weighted_parts, axis=1)
    current = (maxima_all, totals_all, weighted_all)
    bit_count = members.bit_length() - 1
    for bit_index in reversed(range(bit_count)):
        half_rows = current[0].shape[0] // 2
        my_bit = my_index // 2**bit_index % 2
        kept = tuple(
            (
                lax.dynamic_slice_in_dim(part_array, my_bit * half_rows, half_rows, 0)
                for part_array in current
            )
        )
        given = tuple(
            (
                lax.dynamic_slice_in_dim(part_array, (1 - my_bit) * half_rows, half_rows, 0)
                for part_array in current
            )
        )
        partner = swapped((given[0], given[1], given[2]), "ctx", bit_index)
        current = combine(kept, partner)
    finished = (
        (current[2] / current[1][..., None])
        .astype(jnp.bfloat16)
        .reshape(own_rows, ctx_size, per_value_head * HEAD_SIZE)
    )
    returned = lax.all_to_all(finished, "ctx", split_axis=1, concat_axis=1, tiled=True)
    context = (
        returned.reshape(own_rows, kv_heads, members, per_value_head * HEAD_SIZE)
        .transpose(2, 0, 1, 3)
        .reshape(tok_rows, q_heads * HEAD_SIZE)
    )
    handed = passed_along(context, "segment", 1)
    return handed[None]


def solution(mesh):
    return jax.shard_map(
        local,
        mesh=mesh,
        in_specs=(
            P(("groups", "segment"), "ctx", "head"),
            P(("groups", "segment"), "ctx", None, "head"),
            P(("groups", "segment"), "ctx", None, "head"),
            P(("groups", "segment"), None, "head", None),
            P(("groups", "segment")),
        ),
        out_specs=P(("groups", "segment"), "ctx", "head"),
        check_vma=False,
    )
```

profile of v0, /device:TPU:0, one launch (start us, length us, event | category | flops | bytes accessed | tf_op | source)
XLA Modules:
  0.0 683.2 jit_solution(18266838276464011168)
XLA Ops:
  9.7 6.3 all-to-all-start.2
  23.4 18.4 %all-to-all-done.2 = bf16[512,4,256]{0,2,1:T(8,128)(2,1)S(1)} async-done(((bf16[512,4,256]{0,2,1:T(8,128)(2,1)}), bf16[512,4,256]{0,2,1:T(8,128)(2,1)S(1)}, u32[]{:S(2)}, u32[]{:S(2)}) %all-to-all-start.2) | async-done | bytes 1048608 | tf_op jit(solution)/shard_map/all_to_all | solution.py:89
  45.4 14.1 %reshape_squeeze.8 = bf16[8,1,512,2,4,128]{5,4,3,2,0,1:T(4,128)(2,1)} reshape(bf16[1,4096,2,512]{3,2,1,0:T(2,128)(2,1)} %param.7) | data formatting | bytes 16777216 | tf_op jit(solution)/shard_map/reshape;squeeze | solution.py:99
  59.7 19.3 %fusion.16 = bf16[8,512,4,1,2,128]{5,4,1,0,2,3:T(2,128)(2,1)} fusion(pred[8,4]{0,1:T(4,128)(4,1)S(1)} %dynamic-slice_bitcast_fusion, bf16[8,1,512,2,4,128]{5,4,3,2,0,1:T(4,128)(2,1)} %reshape_squeeze.8), kind=kLoop, calls=%fused_computation.29 | loop fusion | flops 4194304 | bytes 16777248 | tf_op jit(solution)/shard_map/jit(_where)/select_n | solution.py:102
  78.9 14.1 %reshape.803 = bf16[4096,4,256]{2,0,1:T(8,128)(2,1)} reshape(bf16[8,512,4,1,2,128]{5,4,1,0,2,3:T(2,128)(2,1)} %fusion.16) | data formatting | bytes 16777216 | tf_op jit(solution)/shard_map/reshape | solution.py:103
  93.1 5.8 all-to-all-start.1
  121.3 160.3 %all-to-all-done.1 = bf16[4096,4,256]{2,0,1:T(8,128)(2,1)} async-done(((bf16[4096,4,256]{2,0,1:T(8,128)(2,1)}), bf16[4096,4,256]{2,0,1:T(8,128)(2,1)}, u32[]{:S(2)}, u32[]{:S(2)}) %all-to-all-start.1) | async-done | bytes 8388640 | tf_op jit(solution)/shard_map/all_to_all | solution.py:104
  281.6 7.5 %copy.91 = bf16[8,512,4,256]{3,1,2,0:T(8,128)(2,1)} copy(bf16[8,512,4,256]{3,1,0,2:T(8,128)(2,1)} %bitcast.6) | data formatting | bytes 16777216 | tf_op jit(solution)/shard_map/reshape | solution.py:105
  305.0 5.4 gather_fusion
  313.9 13.1 %multiply_reduce_fusion.2 = (f32[2048]{0:T(1024)S(1)}, f32[2048,4096]{1,0:T(8,128)}) fusion(bf16[2048,128]{1,0:T(8,128)(2,1)S(1)} %copy-done.11, bf16[4096,128]{1,0:T(8,128)(2,1)S(1)} %bitcast.134), kind=kOutput, calls=%fused_computation.10 | convolution fusion | flops 2164258816 | bytes 35135488 | tf_op jit(solution)/shard_map/dot_general | solution.py:135
  327.0 14.4 %fusion.2 = f32[2048]{0:T(1024)S(1)} fusion(f32[2048,4096]{1,0:T(8,128)} %get-tuple-element.38, f32[2048]{0:T(1024)S(1)} %max.29), kind=kLoop, calls=%fused_computation.14 | loop fusion | flops 25163776 | bytes 33570816 | tf_op jit(solution)/shard_map/reduce_sum | solution.py:145
  341.4 23.2 %fusion.3 = f32[2048,128]{1,0:T(8,128)S(1)} fusion(bf16[4096,128]{1,0:T(8,128)(2,1)S(1)} %bitcast.133, f32[2048,4096]{1,0:T(8,128)} %get-tuple-element.38, f32[2048]{0:T(1024)S(1)} %max.29), kind=kOutput, calls=%fused_computation.15 | convolution fusion | flops 12901679104 | bytes 35659776 | tf_op jit(solution)/shard_map/dot_general | solution.py:146
  372.9 17.0 %multiply_reduce_fusion.3 = (f32[2048]{0:T(1024)S(1)}, f32[2048,4096]{1,0:T(8,128)}) fusion(bf16[2048,128]{1,0:T(8,128)(2,1)} %copy-done.9, bf16[4096,128]{1,0:T(8,128)(2,1)} %bitcast.132), kind=kOutput, calls=%fused_computation.11 | convolution fusion | flops 2164258816 | bytes 35135488 | tf_op jit(solution)/shard_map/dot_general | solution.py:135
  389.9 14.1 %fusion = f32[2048]{0:T(1024)S(1)} fusion(f32[2048,4096]{1,0:T(8,128)} %get-tuple-element.42, f32[2048]{0:T(1024)S(1)} %max.28), kind=kLoop, calls=%fused_computation.12 | loop fusion | flops 25163776 | bytes 33570816 | tf_op jit(solution)/shard_map/reduce_sum | solution.py:145
  404.0 23.4 %fusion.1 = f32[2048,128]{1,0:T(8,128)S(1)} fusion(bf16[4096,128]{1,0:T(8,128)(2,1)S(1)} %bitcast.131, f32[2048,4096]{1,0:T(8,128)} %get-tuple-element.42, f32[2048]{0:T(1024)S(1)} %max.28), kind=kOutput, calls=%fused_computation.13 | convolution fusion | flops 12901679104 | bytes 35659776 | tf_op jit(solution)/shard_map/dot_general | solution.py:146
  438.5 17.0 %multiply_reduce_fusion.1 = (f32[2048]{0:T(1024)S(1)}, f32[2048,4096]{1,0:T(8,128)}) fusion(bf16[2048,128]{1,0:T(8,128)(2,1)} %copy-done.8, bf16[4096,128]{1,0:T(8,128)(2,1)} %bitcast.130), kind=kOutput, calls=%fused_computation.9 | convolution fusion | flops 2164258816 | bytes 35135488 | tf_op jit(solution)/shard_map/dot_general | solution.py:135
  455.5 14.0 %fusion.4 = f32[2048]{0:T(1024)S(1)} fusion(f32[2048,4096]{1,0:T(8,128)} %get-tuple-element.34, f32[2048]{0:T(1024)S(1)} %max.30), kind=kLoop, calls=%fused_computation.16 | loop fusion | flops 25163776 | bytes 33570816 | tf_op jit(solution)/shard_map/reduce_sum | solution.py:145
  469.6 23.8 %fusion.5 = f32[2048,128]{1,0:T(8,128)S(1)} fusion(bf16[4096,128]{1,0:T(8,128)(2,1)} %bitcast.129, f32[2048,4096]{1,0:T(8,128)} %get-tuple-element.34, f32[2048]{0:T(1024)S(1)} %max.30), kind=kOutput, calls=%fused_computation.17 | convolution fusion | flops 12901679104 | bytes 35659776 | tf_op jit(solution)/shard_map/dot_general | solution.py:146
  505.5 17.0 %multiply_reduce_fusion = (f32[2048]{0:T(1024)S(1)}, f32[2048,4096]{1,0:T(8,128)}) fusion(bf16[2048,128]{1,0:T(8,128)(2,1)} %copy-done.7, bf16[4096,128]{1,0:T(8,128)(2,1)} %bitcast.128), kind=kOutput, calls=%fused_computation.8 | convolution fusion | flops 2164258816 | bytes 35135488 | tf_op jit(solution)/shard_map/dot_general | solution.py:135
  522.5 14.0 %fusion.6 = f32[2048]{0:T(1024)S(1)} fusion(f32[2048,4096]{1,0:T(8,128)} %get-tuple-element.30, f32[2048]{0:T(1024)S(1)} %max.31), kind=kLoop, calls=%fused_computation.18 | loop fusion | flops 25163776 | bytes 33570816 | tf_op jit(solution)/shard_map/reduce_sum | solution.py:145
  536.5 23.6 %fusion.7 = f32[2048,128]{1,0:T(8,128)S(1)} fusion(bf16[4096,128]{1,0:T(8,128)(2,1)} %bitcast.127, f32[2048,4096]{1,0:T(8,128)} %get-tuple-element.30, f32[2048]{0:T(1024)S(1)} %max.31), kind=kOutput, calls=%fused_computation.19 | convolution fusion | flops 12901679104 | bytes 35659776 | tf_op jit(solution)/shard_map/dot_general | solution.py:146
  576.5 5.6 div.68
  585.0 50.2 %all_to_all.20 = bf16[512,4,512]{2,0,1:T(8,128)(2,1)S(1)} all-to-all(bf16[512,4,512]{2,0,1:T(8,128)(2,1)S(1)} %fusion.17), channel_id=1, replica_groups=mesh['groups'=2,'ctx'=4,'segment'=2,'head'=2] {'ctx'}, dimensions={1} | all-to-all | bytes 4194304 | tf_op jit(solution)/shard_map/all_to_all | solution.py:182
  637.1 44.6 %collective-permute-done = bf16[512,2048]{1,0:T(8,128)(2,1)S(1)} collective-permute-done((bf16[512,2048]{1,0:T(8,128)(2,1)S(1)}, bf16[512,2048]{1,0:T(8,128)(2,1)S(1)}, u32[]{:S(2)}, u32[]{:S(2)}) %collective-permute-start) | collective-permute-done | bytes 2097184 | tf_op jit(solution)/shard_map/ppermute | solution.py:21
  (108 shorter events, 115.9 us)
Async XLA Ops:
  7.5 8.6 %copy-start.12 = (bf16[1,512,2048]{2,1,0:T(8,128)(2,1)S(1)}, bf16[1,512,2048]{2,1,0:T(8,128)(2,1)}, u32[]{:S(2)}) copy-start(bf16[1,512,2048]{2,1,0:T(8,128)(2,1)} %param.5) | copy-start | bytes 6291460
  9.7 32.1 %all-to-all-start.2 = ((bf16[512,4,256]{0,2,1:T(8,128)(2,1)}), bf16[512,4,256]{0,2,1:T(8,128)(2,1)S(1)}, u32[]{:S(2)}, u32[]{:S(2)}) async-start(bf16[512,4,256]{0,2,1:T(8,128)(2,1)} %pad_maximum_fusion.1), calls=%async_computation.2 | async-start | bytes 2097152 | tf_op jit(solution)/shard_map/all_to_all | solution.py:89
  41.8 76.7 %copy-start.6 = (bf16[512,4,256]{0,2,1:T(8,128)(2,1)}, bf16[512,4,256]{0,2,1:T(8,128)(2,1)S(1)}, u32[]{:S(2)}) copy-start(bf16[512,4,256]{0,2,1:T(8,128)(2,1)S(1)} %all-to-all-done.2) | copy-start | bytes 3145732
  41.8 51.3 %all-to-all-start = ((bf16[512,4,512]{0,2,1:T(8,128)(2,1)}), bf16[512,4,512]{0,2,1:T(8,128)(2,1)S(1)}, u32[]{:S(2)}, u32[]{:S(2)}) async-start(bf16[512,4,512]{0,2,1:T(8,128)(2,1)} %bitcast.124), calls=%async_computation | async-start | bytes 4194304 | tf_op jit(solution)/shard_map/all_to_all | solution.py:88
  45.4 14.1 %copy-start.13 = (s32[1,4,4,8]{3,2,1,0:T(4,128)S(1)}, s32[1,4,4,8]{3,2,1,0:T(4,128)}, u32[]{:S(2)}) copy-start(s32[1,4,4,8]{3,2,1,0:T(4,128)} %param.8) | copy-start | bytes 1540
  93.1 188.5 %all-to-all-start.1 = ((bf16[4096,4,256]{2,0,1:T(8,128)(2,1)}), bf16[4096,4,256]{2,0,1:T(8,128)(2,1)}, u32[]{:S(2)}, u32[]{:S(2)}) async-start(bf16[4096,4,256]{2,0,1:T(8,128)(2,1)} %reshape.803), calls=%async_computation.1 | async-start | bytes 16777216 | tf_op jit(solution)/shard_map/all_to_all | solution.py:104
  103.1 10.0 %copy-start.9 = (bf16[2048,128]{1,0:T(8,128)(2,1)}, bf16[2048,128]{1,0:T(8,128)(2,1)S(1)}, u32[]{:S(2)}) copy-start(bf16[2048,128]{1,0:T(8,128)(2,1)S(1)} %reshape.802) | copy-start | bytes 1572868
  104.9 13.7 %copy-start.7 = (bf16[2048,128]{1,0:T(8,128)(2,1)}, bf16[2048,128]{1,0:T(8,128)(2,1)S(1)}, u32[]{:S(2)}) copy-start(bf16[2048,128]{1,0:T(8,128)(2,1)S(1)} %reshape.819) | copy-start | bytes 1572868
  106.6 9.1 %copy-start.8 = (bf16[2048,128]{1,0:T(8,128)(2,1)}, bf16[2048,128]{1,0:T(8,128)(2,1)S(1)}, u32[]{:S(2)}) copy-start(bf16[2048,128]{1,0:T(8,128)(2,1)S(1)} %reshape.814) | copy-start | bytes 1572868
  110.2 5.5 copy-start.10
  310.4 3.5 copy-start.11
  364.6 3.5 copy-start.3
  389.9 14.1 %copy-start.5 = (bf16[8,512,128]{2,1,0:T(8,128)(2,1)S(1)}, bf16[8,512,128]{2,1,0:T(8,128)(2,1)}, u32[]{:S(2)}) copy-start(bf16[8,512,128]{2,1,0:T(8,128)(2,1)} %get-tuple-element.7) | copy-start | bytes 3145732
  427.4 3.5 copy-start.2
  493.4 3.5 copy-start.1
  560.1 3.5 copy-start
  576.5 5.6 copy-start.4
  635.5 46.2 %collective-permute-start = (bf16[512,2048]{1,0:T(8,128)(2,1)S(1)}, bf16[512,2048]{1,0:T(8,128)(2,1)S(1)}, u32[]{:S(2)}, u32[]{:S(2)}) collective-permute-start(bf16[512,2048]{1,0:T(8,128)(2,1)S(1)} %bitcast.135), channel_id=1, source_target_pairs={{2,0},{0,2},{3,1},{1,3},{6,4},{4,6},{7,5},{5,7},{10,8},{8,10},{11,... | collective-permute-start | bytes 6291464 | tf_op jit(solution)/shard_map/ppermute | solution.py:21
where the time goes:
time: 690 us; the launch traced here: 683 us
  waiting for transfers between devices  223 us (32%)
  matrix products  189 us (27%)
  local copies, waits for them, and re-layouts  102 us (15%)
  other arithmetic  99.2 us (14%)
  blocking collectives  50.2 us (7%)
  starting transfers between devices  17.3 us (3%)
    all_to_all x1, waiting for transfers between devices, local(): lax.all_to_all(tile_send, 'ctx', split_axis=1, concat_axis=1, tiled=True)  160 us
    dot_general x4, matrix products, local(): jnp.dot(sel_weights, sel_values.astype(jnp.float32), precision=lax.Precis...  93.9 us
    reduce_sum x8, other arithmetic, local(): totals = jnp.sum(sel_weights, axis=1) + jnp.sum(own_weights, axis=1)  68.4 us
    dot_general x4, matrix products, local(): jnp.dot(query_rows, sel_keys.T, preferred_element_type=jnp.float32)  64 us
    all_to_all x1, blocking collectives, local(): lax.all_to_all(finished, 'ctx', split_axis=1, concat_axis=1, tiled=True)  50.2 us
    ppermute x1, waiting for transfers between devices, passed_along(): return lax.ppermute(block, axis, route)  44.6 us
    dot_general x4, matrix products, local(): jnp.dot(own_weights, own_values.astype(jnp.float32), precision=lax.Precis...  20.5 us
    select_n x1, other arithmetic, local(): jnp.where(needed_here, arranged_rows, jnp.zeros((), jnp.bfloat16))  19.3 us
  transfers between devices with their start and end apart: 4, of which 4 were waited for; matrix products, arithmetic and copies ran while one was open for 11% of the time, Pallas kernels for 0%

commit v1 on v0

--- a/solution.py
+++ b/solution.py
@@ -1,6 +1,10 @@
+import functools
+
 import jax
 import jax.numpy as jnp
 from jax import lax
+from jax.experimental import pallas as pl
+from jax.experimental.pallas import tpu as pltpu
 from jax.sharding import PartitionSpec as P
 
 HEAD_SIZE = 128
@@ -49,7 +53,7 @@
     return (maxima, totals, weighted)
 
 
-def local(queries, span_key_values, key_value_cache, chosen, offset):
+def general(queries, span_key_values, key_value_cache, chosen, offset):
     ctx_size = lax.axis_size("ctx")
     my_index = lax.axis_index("ctx")
     tok_rows = queries.shape[1]
@@ -189,6 +193,248 @@
     return handed[None]
 
 
+CHUNKS = 4
+LOG2E = 1.4426950408889634
+MESH = pl.DeviceIdType.MESH
+
+
+def attend_kernel(
+    n_ctx,
+    n_seg,
+    chosen_ref,
+    q_ref,
+    span_ref,
+    cache_ref,
+    out_ref,
+    q_buf,
+    span_buf,
+    *rest,
+):
+    kv_bufs = rest[:CHUNKS]
+    (k_cat, v_cat, m_buf, acc, tot, done, q_send, q_recv, s_send, s_recv,
+     c_send, c_recv, own_sem, o_send, o_recv) = rest[CHUNKS:]
+    me = lax.axis_index("ctx")
+    seg = lax.axis_index("segment")
+    blocks_here = cache_ref.shape[2]
+    chunk_rows = cache_ref.shape[4]
+    per_head = q_ref.shape[1]
+    tokens = q_ref.shape[2]
+    after = lax.rem(seg + 1, n_seg)
+    before = lax.rem(seg + n_seg - 1, n_seg)
+    c2 = LOG2E * HEAD_SIZE ** (-0.5)
+
+    barrier = pltpu.get_barrier_semaphore()
+    greeted = 0
+    for step in range(1, n_ctx):
+        pl.semaphore_signal(
+            barrier, inc=1, device_id={"ctx": lax.rem(me + step, n_ctx)}, device_id_type=MESH
+        )
+        greeted += 1
+    for other in (after,) if n_seg == 2 else (after, before):
+        for step in range(n_ctx):
+            pl.semaphore_signal(
+                barrier,
+                inc=1,
+                device_id={"ctx": lax.rem(me + step, n_ctx), "segment": other},
+                device_id_type=MESH,
+            )
+            greeted += 1
+    pl.semaphore_wait(barrier, greeted)
+
+    def to(step):
+        return lax.rem(me + step, n_ctx)
+
+    def remote(source, target, send, recv, step):
+        return pltpu.make_async_remote_copy(
+            src_ref=source,
+            dst_ref=target,
+            send_sem=send,
+            recv_sem=recv,
+            device_id={"ctx": to(step)},
+            device_id_type=MESH,
+        )
+
+    steps = [s for s in (2, 1, 3) if s < n_ctx] + list(range(4, n_ctx))
+    mine = pl.ds(me * blocks_here, blocks_here)
+    q_copies = [remote(q_ref.at[to(s)], q_buf.at[me], q_send.at[s], q_recv.at[s], s) for s in steps]
+    s_copies = [
+        remote(span_ref.at[to(s)], span_buf.at[me], s_send.at[s], s_recv.at[s], s) for s in steps
+    ]
+    c_copies = [
+        [
+            remote(
+                cache_ref.at[c, to(s)], kv_bufs[c].at[mine], c_send.at[c, s], c_recv.at[c, s], s
+            )
+            for s in steps
+        ]
+        for c in range(CHUNKS)
+    ]
+    own_copies = [
+        pltpu.make_async_copy(q_ref.at[me], q_buf.at[me], own_sem.at[CHUNKS]),
+        pltpu.make_async_copy(span_ref.at[me], span_buf.at[me], own_sem.at[CHUNKS + 1]),
+    ] + [
+        pltpu.make_async_copy(cache_ref.at[c, me], kv_bufs[c].at[mine], own_sem.at[c])
+        for c in range(CHUNKS)
+    ]
+    for copy in q_copies + s_copies:
+        copy.start()
+    for copies in c_copies:
+        for copy in copies:
+            copy.start()
+    for copy in own_copies:
+        copy.start()
+
+    v_cat[:, HEAD_SIZE:] = jnp.ones((v_cat.shape[0], HEAD_SIZE), v_cat.dtype)
+
+    def fold(b, h, keys, values, causal, first):
+        scores = lax.dot_general(
+            q_buf[b, h], keys, (((1,), (1,)), ((), ())), preferred_element_type=jnp.float32
+        )
+        if causal is not None:
+            scores = jnp.where(causal, scores, -jnp.inf)
+        top = jnp.broadcast_to(jnp.max(scores, axis=1, keepdims=True), (tokens, HEAD_SIZE))
+        if not first:
+            held = m_buf[b, h]
+            top = jnp.maximum(top, held)
+        wide = jnp.concatenate([top] * (scores.shape[1] // HEAD_SIZE), axis=1)
+        weights = jnp.exp2((scores - wide) * c2).astype(jnp.bfloat16)
+        part = jnp.dot(weights, values, preferred_element_type=jnp.float32)
+        if first:
+            acc[b, h] = part[:, :HEAD_SIZE]
+            tot[b, h] = part[:, HEAD_SIZE:]
+        else:
+            factor = jnp.exp2((held - top) * c2)
+            acc[b, h] = acc[b, h] * factor + part[:, :HEAD_SIZE]
+            tot[b, h] = tot[b, h] * factor + part[:, HEAD_SIZE:]
+        m_buf[b, h] = top
+
+    for copy in q_copies + s_copies:
+        copy.wait_recv()
+    own_copies[0].wait()
+    own_copies[1].wait()
+
+    @pl.loop(0, n_ctx)
+    def _(b):
+        v_cat[:tokens, :HEAD_SIZE] = span_buf[b, 1]
+        rows = lax.broadcasted_iota(jnp.int32, (tokens, tokens), 0)
+        columns = lax.broadcasted_iota(jnp.int32, (tokens, tokens), 1)
+
+        @pl.loop(0, per_head)
+        def _(h):
+            fold(b, h, span_buf[b, 0], v_cat[:tokens], columns <= rows, True)
+
+    def gather(c, b):
+        for n in range(CHOSEN_BLOCKS):
+            block = chosen_ref[(b * n_ctx + me) * CHOSEN_BLOCKS + n]
+            spot = slice(n * chunk_rows, (n + 1) * chunk_rows)
+            k_cat[spot, :] = kv_bufs[c][block, 0]
+            v_cat[spot, :HEAD_SIZE] = kv_bufs[c][block, 1]
+
+    def out_copy(step):
+        return pltpu.make_async_remote_copy(
+            src_ref=done.at[step],
+            dst_ref=out_ref.at[0, :, pl.ds(pl.multiple_of(me * per_head * HEAD_SIZE, HEAD_SIZE), per_head * HEAD_SIZE)],
+            send_sem=o_send.at[step],
+            recv_sem=o_recv.at[step],
+            device_id={"ctx": to(step), "segment": after},
+            device_id_type=MESH,
+        )
+
+    for c in range(CHUNKS):
+        for copy in c_copies[c]:
+            copy.wait_recv()
+        own_copies[2 + c].wait()
+        if c < CHUNKS - 1:
+
+            @pl.loop(0, n_ctx)
+            def _(b):
+                gather(c, b)
+
+                @pl.loop(0, per_head)
+                def _(h):
+                    fold(b, h, k_cat[...], v_cat[...], None, False)
+
+        else:
+
+            @pl.loop(0, n_ctx)
+            def _(i):
+                step = lax.rem(i + 2, n_ctx)
+                b = to(step)
+                gather(c, b)
+                for h in range(per_head):
+                    fold(b, h, k_cat[...], v_cat[...], None, False)
+                    done[step, :, h * HEAD_SIZE : (h + 1) * HEAD_SIZE] = (
+                        acc[b, h] / tot[b, h]
+                    ).astype(done.dtype)
+                out_copy(step).start()
+
+    for copies in [q_copies, s_copies] + c_copies:
+        for copy in copies:
+            copy.wait_send()
+    for step in range(n_ctx):
+        out_copy(step).wait()
+
+
+def local(queries, span_key_values, key_value_cache, chosen, offset):
+    n_ctx = lax.axis_size("ctx")
+    n_seg = lax.axis_size("segment")
+    me = lax.axis_index("ctx")
+    tokens = queries.shape[1]
+    kv_heads = key_value_cache.shape[3] // HEAD_SIZE
+    q_heads = queries.shape[2] // HEAD_SIZE
+    per_head = q_heads // kv_heads
+    if not (n_ctx == kv_heads and tokens == BLOCK_TOKENS and n_seg > 1):
+        return general(queries, span_key_values, key_value_cache, chosen, offset)
+    blocks_here = key_value_cache.shape[1] // BLOCK_TOKENS
+    blocks = blocks_here * n_ctx
+    chunk_rows = BLOCK_TOKENS // CHUNKS
+    positions = (offset[0] + me * tokens + jnp.arange(tokens, dtype=jnp.int32)).astype(jnp.float32)
+    rot_query = apply_rotary(queries[0].reshape(tokens, q_heads, HEAD_SIZE), positions)
+    rot_keys = apply_rotary(span_key_values[0, :, 0].reshape(tokens, kv_heads, HEAD_SIZE), positions)
+    values = span_key_values[0, :, 1].reshape(tokens, kv_heads, HEAD_SIZE)
+    q_send = rot_query.transpose(1, 0, 2).reshape(kv_heads, per_head, tokens, HEAD_SIZE)
+    span_send = jnp.stack([rot_keys.transpose(1, 0, 2), values.transpose(1, 0, 2)], axis=1)
+    cache_send = (
+        key_value_cache[0]
+        .reshape(blocks_here, CHUNKS, chunk_rows, 2, kv_heads, HEAD_SIZE)
+        .transpose(1, 4, 0, 3, 2, 5)
+    )
+    bf16, f32 = jnp.bfloat16, jnp.float32
+    dma = pltpu.SemaphoreType.DMA
+    gathered = CHOSEN_BLOCKS * chunk_rows
+    return pl.pallas_call(
+        functools.partial(attend_kernel, n_ctx, n_seg),
+        out_shape=jax.ShapeDtypeStruct(queries.shape, bf16),
+        in_specs=[pl.BlockSpec(memory_space=pltpu.SMEM)] + [pl.BlockSpec(memory_space=pl.ANY)] * 3,
+        out_specs=pl.BlockSpec(memory_space=pl.ANY),
+        scratch_shapes=[
+            pltpu.VMEM((n_ctx, per_head, tokens, HEAD_SIZE), bf16),
+            pltpu.VMEM((n_ctx, 2, tokens, HEAD_SIZE), bf16),
+        ]
+        + [pltpu.VMEM((blocks, 2, chunk_rows, HEAD_SIZE), bf16)] * CHUNKS
+        + [
+            pltpu.VMEM((gathered, HEAD_SIZE), bf16),
+            pltpu.VMEM((max(gathered, tokens), 2 * HEAD_SIZE), bf16),
+            pltpu.VMEM((n_ctx, per_head, tokens, HEAD_SIZE), f32),
+            pltpu.VMEM((n_ctx, per_head, tokens, HEAD_SIZE), f32),
+            pltpu.VMEM((n_ctx, per_head, tokens, HEAD_SIZE), f32),
+            pltpu.VMEM((n_ctx, tokens, per_head * HEAD_SIZE), bf16),
+            dma((n_ctx,)),
+            dma((n_ctx,)),
+            dma((n_ctx,)),
+            dma((n_ctx,)),
+            dma((CHUNKS, n_ctx)),
+            dma((CHUNKS, n_ctx)),
+            dma((CHUNKS + 2,)),
+            dma((n_ctx,)),
+            dma((n_ctx,)),
+        ],
+        compiler_params=pltpu.CompilerParams(
+            collective_id=0, has_side_effects=True, vmem_limit_bytes=56 * 2**20
+        ),
+    )(chosen.reshape(-1), q_send, span_send, cache_send)
+
+
 def solution(mesh):
     return jax.shard_map(
         local,

time: 690 us -> 360 us (0.52)
  Pallas kernels: 0 us -> 307 us
  waiting for transfers between devices: 223 us -> 0 us
  matrix products: 189 us -> 0 us
  other arithmetic: 99.2 us -> 10.2 us
  local copies, waits for them, and re-layouts: 102 us -> 40.5 us
  blocking collectives: 50.2 us -> 0 us
  starting transfers between devices: 17.3 us -> 0 us
    pallas_call x0 -> x1, Pallas kernels: none -> 307 us  [local(): pl.pallas_call(functools.partial(attend_kernel, n_ctx, n_seg), out_shape=...]
    dot_general x16 -> x0, matrix products: 189 us -> none  [the longest x4 93.9 us: local(): jnp.dot(sel_weights, sel_values.astype(jnp.float32), precision=lax.Precis...]
    all_to_all x3 -> x0, waiting for transfers between devices: 179 us -> none  [the longest x1 160 us: local(): lax.all_to_all(tile_send, 'ctx', split_axis=1, concat_axis=1, tiled=True)]
    reduce_sum x8 -> x0, other arithmetic: 68.4 us -> none  [local(): totals = jnp.sum(sel_weights, axis=1) + jnp.sum(own_weights, axis=1)]
    all_to_all x1 -> x0, blocking collectives: 50.2 us -> none  [local(): lax.all_to_all(finished, 'ctx', split_axis=1, concat_axis=1, tiled=True)]
    ppermute x1 -> x0, waiting for transfers between devices: 44.6 us -> none  [passed_along(): return lax.ppermute(block, axis, route)]
    reshape x6 -> x1, local copies, waits for them, and re-layouts: 23.9 us -> 0.58 us  [local(): chosen.reshape(-1)]
    select_n x1 -> x0, other arithmetic: 19.3 us -> none  [local(): jnp.where(needed_here, arranged_rows, jnp.zeros((), jnp.bfloat16))]
  transfers between devices with their start and end apart: 4 -> 0, of which waited for: 4 -> 0; matrix products, arithmetic and copies ran while one was open for 11% -> 0% of each run, Pallas kernels for 0% -> 0%
where the time goes in v1:
time: 360 us; the launch traced here: 358 us
  Pallas kernels  307 us (85%)
  local copies, waits for them, and re-layouts  40.5 us (11%)
  other arithmetic  10.2 us (3%)
    pallas_call x1, Pallas kernels, local(): pl.pallas_call(functools.partial(attend_kernel, n_ctx, n_seg), out_shape=...  307 us
    another operation x2, local copies, waits for them, and re-layouts, local(): cache_send = key_value_cache[0].reshape(blocks_here, CHUNKS, chunk_rows,...  23.1 us
    unnamed x14, local copies, waits for them, and re-layouts  9.81 us

profile of v1, /device:TPU:0, one launch (start us, length us, event | category | flops | bytes accessed | tf_op | source)
XLA Modules:
  0.0 358.1 jit_solution(14822585014177317412)
XLA Ops:
  0.0 3.5 fusion.1
  3.5 1.3 copy.21
  4.8 0.9 fusion.2
  5.7 0.3 copy.22
  6.1 1.4 copy.23
  8.1 1.0 multiply_cosine_fusion
  9.1 0.0 copy-start
  9.1 0.3 subtract_convert_fusion.1
  9.4 0.4 copy-done
  9.8 1.1 maximum_bitcast_fusion
  10.9 2.3 copy.24
  13.2 1.3 copy.14
  14.5 2.1 pad_maximum_fusion.1.span_ref
  16.6 0.5 convert_bitcast_fusion
  17.2 0.9 copy.25
  18.1 1.3 fusion
  19.5 2.7 subtract_convert_fusion
  22.2 2.5 pad_maximum_fusion
  24.7 14.1 %reshape.73 = bf16[8,4,128,2,4,128]{5,4,3,2,1,0:T(4,128)(2,1)} reshape(bf16[1,4096,2,512]{3,2,1,0:T(2,128)(2,1)} %param.7) | data formatting | bytes 16777216 | tf_op jit(solution)/shard_map/reshape;squeeze | solution.py:399
  38.8 9.0 %copy.31 = bf16[8,4,128,2,4,128]{5,2,3,0,4,1:T(8,128)(2,1)} copy(bf16[8,4,128,2,4,128]{5,4,3,2,1,0:T(4,128)(2,1)} %reshape.73) | data formatting | bytes 16777216 | tf_op jit(solution)/shard_map/reshape;squeeze | solution.py:399
  47.8 0.0 copy-done.3
  47.8 0.6 reshape.69.chosen_ref
  48.4 306.6 %shard_map.55 = bf16[1,512,2048]{2,1,0:T(8,128)(2,1)} custom-call(s32[128]{0:T(128)} %reshape.69.chosen_ref, bf16[4,4,512,128]{3,2,1,0:T(8,128)(2,1)} %bitcast.24, bf16[4,2,512,128]{3,2,1,0:T(8,128)(2,1)} %pad_maximum_fusion.1.span_ref, bf16[4,4,8,2,128,128]{5,4,3,2,1,0:T(8,128)(2,1)} %bitcast.23), custom_call_target="tpu_custom_call" | custom-call | tf_op jit(solution)/shard_map/pallas_call | solution.py:405
  355.0 3.2 copy.34
  (7 shorter events, 0.0 us)
Async XLA Ops:
  9.1 0.7 copy-start
  9.8 6.8 %copy-start.2 = (bf16[1,512,2048]{2,1,0:T(8,128)(2,1)S(1)}, bf16[1,512,2048]{2,1,0:T(8,128)(2,1)}, u32[]{:S(2)}) copy-start(bf16[1,512,2048]{2,1,0:T(8,128)(2,1)} %param.5) | copy-start | bytes 6291460
  18.1 1.4 copy-start.1
  38.8 9.0 %copy-start.3 = (s32[1,4,4,8]{3,2,1,0:T(4,128)S(1)}, s32[1,4,4,8]{3,2,1,0:T(4,128)}, u32[]{:S(2)}) copy-start(s32[1,4,4,8]{3,2,1,0:T(4,128)} %param.8) | copy-start | bytes 1540

commit v2 on v1

--- a/solution.py
+++ b/solution.py
@@ -202,6 +202,8 @@
     n_ctx,
     n_seg,
     chosen_ref,
+    cos_ref,
+    sin_ref,
     q_ref,
     span_ref,
     cache_ref,
@@ -211,14 +213,14 @@
     *rest,
 ):
     kv_bufs = rest[:CHUNKS]
-    (k_cat, v_cat, m_buf, acc, tot, done, q_send, q_recv, s_send, s_recv,
+    (k_cat, v_cat, m_buf, acc, tot, done, q_sem, s_send, s_recv,
      c_send, c_recv, own_sem, o_send, o_recv) = rest[CHUNKS:]
     me = lax.axis_index("ctx")
     seg = lax.axis_index("segment")
     blocks_here = cache_ref.shape[2]
     chunk_rows = cache_ref.shape[4]
-    per_head = q_ref.shape[1]
-    tokens = q_ref.shape[2]
+    per_head = q_ref.shape[2] // HEAD_SIZE
+    tokens = q_ref.shape[1]
     after = lax.rem(seg + 1, n_seg)
     before = lax.rem(seg + n_seg - 1, n_seg)
     c2 = LOG2E * HEAD_SIZE ** (-0.5)
@@ -256,7 +258,13 @@
 
     steps = [s for s in (2, 1, 3) if s < n_ctx] + list(range(4, n_ctx))
     mine = pl.ds(me * blocks_here, blocks_here)
-    q_copies = [remote(q_ref.at[to(s)], q_buf.at[me], q_send.at[s], q_recv.at[s], s) for s in steps]
+    q_copies = [
+        pltpu.make_async_copy(
+            q_ref.at[b, :, pl.ds(h * HEAD_SIZE, HEAD_SIZE)], q_buf.at[b, h], q_sem.at[b, h]
+        )
+        for b in range(n_ctx)
+        for h in range(per_head)
+    ]
     s_copies = [
         remote(span_ref.at[to(s)], span_buf.at[me], s_send.at[s], s_recv.at[s], s) for s in steps
     ]
@@ -270,18 +278,17 @@
         for c in range(CHUNKS)
     ]
     own_copies = [
-        pltpu.make_async_copy(q_ref.at[me], q_buf.at[me], own_sem.at[CHUNKS]),
-        pltpu.make_async_copy(span_ref.at[me], span_buf.at[me], own_sem.at[CHUNKS + 1]),
+        pltpu.make_async_copy(span_ref.at[me], span_buf.at[me], own_sem.at[CHUNKS]),
     ] + [
         pltpu.make_async_copy(cache_ref.at[c, me], kv_bufs[c].at[mine], own_sem.at[c])
         for c in range(CHUNKS)
     ]
-    for copy in q_copies + s_copies:
+    for copy in s_copies:
         copy.start()
     for copies in c_copies:
         for copy in copies:
             copy.start()
-    for copy in own_copies:
+    for copy in q_copies + own_copies:
         copy.start()
 
     v_cat[:, HEAD_SIZE:] = jnp.ones((v_cat.shape[0], HEAD_SIZE), v_cat.dtype)
@@ -308,20 +315,34 @@
             tot[b, h] = tot[b, h] * factor + part[:, HEAD_SIZE:]
         m_buf[b, h] = top
 
-    for copy in q_copies + s_copies:
+    def rotated(block, b):
+        wide = block.astype(jnp.float32)
+        turned = pltpu.roll(wide, HEAD_SIZE // 2, 1)
+        return (wide * cos_ref[b] + turned * sin_ref[b]).astype(jnp.bfloat16)
+
+    for copy in q_copies:
+        copy.wait()
+
+    @pl.loop(0, n_ctx)
+    def _(b):
+        @pl.loop(0, per_head)
+        def _(h):
+            q_buf[b, h] = rotated(q_buf[b, h], b)
+
+    for copy in s_copies:
         copy.wait_recv()
     own_copies[0].wait()
-    own_copies[1].wait()
 
     @pl.loop(0, n_ctx)
     def _(b):
+        k_cat[:tokens, :] = rotated(span_buf[b, 0], b)
         v_cat[:tokens, :HEAD_SIZE] = span_buf[b, 1]
         rows = lax.broadcasted_iota(jnp.int32, (tokens, tokens), 0)
         columns = lax.broadcasted_iota(jnp.int32, (tokens, tokens), 1)
 
         @pl.loop(0, per_head)
         def _(h):
-            fold(b, h, span_buf[b, 0], v_cat[:tokens], columns <= rows, True)
+            fold(b, h, k_cat[:tokens], v_cat[:tokens], columns <= rows, True)
 
     def gather(c, b):
         for n in range(CHOSEN_BLOCKS):
@@ -343,7 +364,7 @@
     for c in range(CHUNKS):
         for copy in c_copies[c]:
             copy.wait_recv()
-        own_copies[2 + c].wait()
+        own_copies[1 + c].wait()
         if c < CHUNKS - 1:
 
             @pl.loop(0, n_ctx)
@@ -368,7 +389,7 @@
                     ).astype(done.dtype)
                 out_copy(step).start()
 
-    for copies in [q_copies, s_copies] + c_copies:
+    for copies in [s_copies] + c_copies:
         for copy in copies:
             copy.wait_send()
     for step in range(n_ctx):
@@ -378,7 +399,6 @@
 def local(queries, span_key_values, key_value_cache, chosen, offset):
     n_ctx = lax.axis_size("ctx")
     n_seg = lax.axis_size("segment")
-    me = lax.axis_index("ctx")
     tokens = queries.shape[1]
     kv_heads = key_value_cache.shape[3] // HEAD_SIZE
     q_heads = queries.shape[2] // HEAD_SIZE
@@ -388,12 +408,21 @@
     blocks_here = key_value_cache.shape[1] // BLOCK_TOKENS
     blocks = blocks_here * n_ctx
     chunk_rows = BLOCK_TOKENS // CHUNKS
-    positions = (offset[0] + me * tokens + jnp.arange(tokens, dtype=jnp.int32)).astype(jnp.float32)
-    rot_query = apply_rotary(queries[0].reshape(tokens, q_heads, HEAD_SIZE), positions)
-    rot_keys = apply_rotary(span_key_values[0, :, 0].reshape(tokens, kv_heads, HEAD_SIZE), positions)
-    values = span_key_values[0, :, 1].reshape(tokens, kv_heads, HEAD_SIZE)
-    q_send = rot_query.transpose(1, 0, 2).reshape(kv_heads, per_head, tokens, HEAD_SIZE)
-    span_send = jnp.stack([rot_keys.transpose(1, 0, 2), values.transpose(1, 0, 2)], axis=1)
+    q_all = lax.all_to_all(
+        queries[0].reshape(tokens, n_ctx, per_head * HEAD_SIZE).transpose(1, 0, 2),
+        "ctx",
+        split_axis=0,
+        concat_axis=0,
+        tiled=True,
+    )
+    positions = (offset[0] + jnp.arange(n_ctx * tokens, dtype=jnp.int32)).astype(jnp.float32)
+    half = HEAD_SIZE // 2
+    frequencies = ROPE_BASE ** (-(2.0 * jnp.arange(half, dtype=jnp.float32)) / HEAD_SIZE)
+    angles = positions[:, None] * frequencies[None, :]
+    cosine, sine = jnp.cos(angles), jnp.sin(angles)
+    cos_table = jnp.concatenate([cosine, cosine], axis=1).reshape(n_ctx, tokens, HEAD_SIZE)
+    sin_table = jnp.concatenate([-sine, sine], axis=1).reshape(n_ctx, tokens, HEAD_SIZE)
+    span_send = span_key_values[0].reshape(tokens, 2, kv_heads, HEAD_SIZE).transpose(2, 1, 0, 3)
     cache_send = (
         key_value_cache[0]
         .reshape(blocks_here, CHUNKS, chunk_rows, 2, kv_heads, HEAD_SIZE)
@@ -405,7 +434,9 @@
     return pl.pallas_call(
         functools.partial(attend_kernel, n_ctx, n_seg),
         out_shape=jax.ShapeDtypeStruct(queries.shape, bf16),
-        in_specs=[pl.BlockSpec(memory_space=pltpu.SMEM)] + [pl.BlockSpec(memory_space=pl.ANY)] * 3,
+        in_specs=[pl.BlockSpec(memory_space=pltpu.SMEM)]
+        + [pl.BlockSpec(memory_space=pltpu.VMEM)] * 2
+        + [pl.BlockSpec(memory_space=pl.ANY)] * 3,
         out_specs=pl.BlockSpec(memory_space=pl.ANY),
         scratch_shapes=[
             pltpu.VMEM((n_ctx, per_head, tokens, HEAD_SIZE), bf16),
@@ -419,20 +450,19 @@
             pltpu.VMEM((n_ctx, per_head, tokens, HEAD_SIZE), f32),
             pltpu.VMEM((n_ctx, per_head, tokens, HEAD_SIZE), f32),
             pltpu.VMEM((n_ctx, tokens, per_head * HEAD_SIZE), bf16),
-            dma((n_ctx,)),
-            dma((n_ctx,)),
+            dma((n_ctx, per_head)),
             dma((n_ctx,)),
             dma((n_ctx,)),
             dma((CHUNKS, n_ctx)),
             dma((CHUNKS, n_ctx)),
-            dma((CHUNKS + 2,)),
+            dma((CHUNKS + 1,)),
             dma((n_ctx,)),
             dma((n_ctx,)),
         ],
         compiler_params=pltpu.CompilerParams(
             collective_id=0, has_side_effects=True, vmem_limit_bytes=56 * 2**20
         ),
-    )(chosen.reshape(-1), q_send, span_send, cache_send)
+    )(chosen.reshape(-1), cos_table, sin_table, q_all, span_send, cache_send)
 
 
 def solution(mesh):

time: 360 us -> 325 us (0.903)
  Pallas kernels: 307 us -> 259 us
  waiting for transfers between devices: 0 us -> 14.2 us
  starting transfers between devices: 0 us -> 6.35 us
  other arithmetic: 10.2 us -> 5.76 us
    pallas_call x1, Pallas kernels: 307 us -> 259 us  [local(): pl.pallas_call(functools.partial(attend_kernel, n_ctx, n_seg), out_shape=...]
    all_to_all x0 -> x1, waiting for transfers between devices: none -> 14.2 us  [local(): lax.all_to_all(queries[0].reshape(tokens, n_ctx, per_head * HEAD_SIZE).tr...]
    all_to_all x0 -> x1, starting transfers between devices: none -> 6.35 us  [local(): lax.all_to_all(queries[0].reshape(tokens, n_ctx, per_head * HEAD_SIZE).tr...]
    another operation x4 -> x0, other arithmetic: 6.22 us -> none  [the longest x2 3.2 us: local(): jnp.stack([rot_keys.transpose(1, 0, 2), values.transpose(1, 0, 2)], axis=1)]
    slice x3 -> x0, local copies, waits for them, and re-layouts: 5.74 us -> none  [the longest x1 3.47 us: local(): span_key_values[0, :, 0].reshape(tokens, kv_heads, HEAD_SIZE)]
    neg x0 -> x1, other arithmetic: none -> 3.72 us  [local(): -sine]
    unnamed x14 -> x7, local copies, waits for them, and re-layouts: 9.81 us -> 9.8 us
  transfers between devices with their start and end apart: 0 -> 1, of which waited for: 0 -> 1; matrix products, arithmetic and copies ran while one was open for 0% -> 10% of each run, Pallas kernels for 0% -> 0%
where the time goes in v2:
time: 325 us; the launch traced here: 323 us
  Pallas kernels  259 us (80%)
  local copies, waits for them, and re-layouts  37.2 us (11%)
  waiting for transfers between devices  14.2 us (4%)
  starting transfers between devices  6.35 us (2%)
  other arithmetic  5.76 us (2%)
    pallas_call x1, Pallas kernels, local(): pl.pallas_call(functools.partial(attend_kernel, n_ctx, n_seg), out_shape=...  259 us
    another operation x2, local copies, waits for them, and re-layouts, local(): cache_send = key_value_cache[0].reshape(blocks_here, CHUNKS, chunk_rows,...  23.1 us
    all_to_all x1, waiting for transfers between devices, local(): lax.all_to_all(queries[0].reshape(tokens, n_ctx, per_head * HEAD_SIZE).tr...  14.2 us
    unnamed x7, local copies, waits for them, and re-layouts  9.8 us
  transfers between devices with their start and end apart: 1, of which 1 were waited for; matrix products, arithmetic and copies ran while one was open for 10% of the time, Pallas kernels for 0%

profile of v2, /device:TPU:0, one launch (start us, length us, event | category | flops | bytes accessed | tf_op | source)
XLA Modules:
  0.0 323.0 jit_solution(12891194237722934677)
XLA Ops:
  0.0 2.9 copy.6
  2.9 2.4 copy.7
  5.2 6.3 %all-to-all-start = ((bf16[4,512,512]{2,1,0:T(8,128)(2,1)}), bf16[4,512,512]{2,1,0:T(8,128)(2,1)S(1)}, u32[]{:S(2)}, u32[]{:S(2)}) async-start(bf16[4,512,512]{2,1,0:T(8,128)(2,1)} %bitcast.10), calls=%async_computation | async-start | bytes 4194304 | tf_op jit(solution)/shard_map/all_to_all | solution.py:411
  12.2 14.1 %reshape.62 = bf16[8,4,128,2,4,128]{5,4,3,2,1,0:T(4,128)(2,1)} reshape(bf16[1,4096,2,512]{3,2,1,0:T(2,128)(2,1)} %param.7) | data formatting | bytes 16777216 | tf_op jit(solution)/shard_map/reshape;squeeze | solution.py:428
  26.3 9.0 %copy.15 = bf16[8,4,128,2,4,128]{5,2,3,0,4,1:T(8,128)(2,1)} copy(bf16[8,4,128,2,4,128]{5,4,3,2,1,0:T(4,128)(2,1)} %reshape.62) | data formatting | bytes 16777216 | tf_op jit(solution)/shard_map/reshape;squeeze | solution.py:428
  35.3 0.0 copy-start.1
  35.3 2.5 copy.8
  37.8 1.3 copy.9
  39.1 0.0 copy-done.1
  39.1 0.7 reshape.61.chosen_ref
  39.8 3.7 %fusion = (f32[4,512,64]{2,1,0:T(8,128)S(1)}, f32[4,512,64]{2,1,0:T(8,128)S(1)}, f32[4,512,64]{2,1,0:T(8,128)S(1)}) fusion(f32[64]{0:T(128)S(1)} %multiply_power_fusion, f32[4,512]{1,0:T(4,128)S(1)} %add_convert_fusion), kind=kLoop, calls=%fused_computation.5 | loop fusion | flops 262144 | bytes 1581312 | tf_op jit(solution)/shard_map/neg | solution.py:424
  43.5 2.0 pad_maximum_fusion
  45.5 14.2 %all-to-all-done.q_ref = bf16[4,512,512]{2,1,0:T(8,128)(2,1)S(1)} async-done(((bf16[4,512,512]{2,1,0:T(8,128)(2,1)}), bf16[4,512,512]{2,1,0:T(8,128)(2,1)S(1)}, u32[]{:S(2)}, u32[]{:S(2)}) %all-to-all-start) | async-done | bytes 2097184 | tf_op jit(solution)/shard_map/all_to_all | solution.py:411
  59.8 0.0 copy-start
  59.8 1.3 copy-done
  61.1 258.8 %shard_map.55 = bf16[1,512,2048]{2,1,0:T(8,128)(2,1)} custom-call(s32[128]{0:T(128)} %reshape.61.chosen_ref, f32[4,512,128]{2,1,0:T(8,128)} %get-tuple-element.8.cos_ref, f32[4,512,128]{2,1,0:T(8,128)} %get-tuple-element.9.sin_ref, bf16[4,512,512]{2,1,0:T(8,128)(2,1)} %copy-done, bf16[4,2,512,128]{3,2,1,0:T(8,128)(2,1)} %bitcast.12, ...), custom_call_target="tpu_custom_call" | custom-call | tf_op jit(solution)/shard_map/pallas_call | solution.py:434
  319.9 3.2 copy.18
  (2 shorter events, 0.0 us)
Async XLA Ops:
  5.2 54.5 %all-to-all-start = ((bf16[4,512,512]{2,1,0:T(8,128)(2,1)}), bf16[4,512,512]{2,1,0:T(8,128)(2,1)S(1)}, u32[]{:S(2)}, u32[]{:S(2)}) async-start(bf16[4,512,512]{2,1,0:T(8,128)(2,1)} %bitcast.10), calls=%async_computation | async-start | bytes 4194304 | tf_op jit(solution)/shard_map/all_to_all | solution.py:411
  35.3 3.8 %copy-start.1 = (s32[1,4,4,8]{3,2,1,0:T(4,128)S(1)}, s32[1,4,4,8]{3,2,1,0:T(4,128)}, u32[]{:S(2)}) copy-start(s32[1,4,4,8]{3,2,1,0:T(4,128)} %param.8) | copy-start | bytes 1540
  59.8 1.3 copy-start

commit v3 on v2

--- a/solution.py
+++ b/solution.py
@@ -193,7 +193,7 @@
     return handed[None]
 
 
-CHUNKS = 4
+CHUNKS = 8
 LOG2E = 1.4426950408889634
 MESH = pl.DeviceIdType.MESH
 

time: 325 us -> 324 us (level)
  no operation moved by 1% of the time
where the time goes in v3:
time: 324 us; the launch traced here: 323 us
  Pallas kernels  259 us (80%)
  local copies, waits for them, and re-layouts  37.3 us (12%)
  waiting for transfers between devices  14.2 us (4%)
  starting transfers between devices  6.35 us (2%)
  other arithmetic  5.76 us (2%)
    pallas_call x1, Pallas kernels, local(): pl.pallas_call(functools.partial(attend_kernel, n_ctx, n_seg), out_shape=...  259 us
    another operation x2, local copies, waits for them, and re-layouts, local(): cache_send = key_value_cache[0].reshape(blocks_here, CHUNKS, chunk_rows,...  23.1 us
    all_to_all x1, waiting for transfers between devices, local(): lax.all_to_all(queries[0].reshape(tokens, n_ctx, per_head * HEAD_SIZE).tr...  14.2 us
    unnamed x7, local copies, waits for them, and re-layouts  9.8 us
  transfers between devices with their start and end apart: 1, of which 1 were waited for; matrix products, arithmetic and copies ran while one was open for 10% of the time, Pallas kernels for 0%

profile of v3, /device:TPU:0, one launch (start us, length us, event | category | flops | bytes accessed | tf_op | source)
XLA Modules:
  0.0 323.0 jit_solution(15186886711410366897)
XLA Ops:
  0.0 2.9 copy.6
  2.9 2.4 copy.7
  5.2 6.3 %all-to-all-start = ((bf16[4,512,512]{2,1,0:T(8,128)(2,1)}), bf16[4,512,512]{2,1,0:T(8,128)(2,1)S(1)}, u32[]{:S(2)}, u32[]{:S(2)}) async-start(bf16[4,512,512]{2,1,0:T(8,128)(2,1)} %bitcast.10), calls=%async_computation | async-start | bytes 4194304 | tf_op jit(solution)/shard_map/all_to_all | solution.py:411
  12.2 14.1 %reshape.62 = bf16[8,8,64,2,4,128]{5,4,3,2,1,0:T(4,128)(2,1)} reshape(bf16[1,4096,2,512]{3,2,1,0:T(2,128)(2,1)} %param.7) | data formatting | bytes 16777216 | tf_op jit(solution)/shard_map/reshape;squeeze | solution.py:428
  26.3 9.0 %copy.15 = bf16[8,8,64,2,4,128]{5,2,3,0,4,1:T(8,128)(2,1)} copy(bf16[8,8,64,2,4,128]{5,4,3,2,1,0:T(4,128)(2,1)} %reshape.62) | data formatting | bytes 16777216 | tf_op jit(solution)/shard_map/reshape;squeeze | solution.py:428
  35.4 0.0 copy-start.1
  35.4 2.5 copy.8
  37.8 1.3 copy.9
  39.1 0.0 copy-done.1
  39.1 0.7 reshape.61.chosen_ref
  39.8 3.7 %fusion = (f32[4,512,64]{2,1,0:T(8,128)S(1)}, f32[4,512,64]{2,1,0:T(8,128)S(1)}, f32[4,512,64]{2,1,0:T(8,128)S(1)}) fusion(f32[64]{0:T(128)S(1)} %multiply_power_fusion, f32[4,512]{1,0:T(4,128)S(1)} %add_convert_fusion), kind=kLoop, calls=%fused_computation.5 | loop fusion | flops 262144 | bytes 1581312 | tf_op jit(solution)/shard_map/neg | solution.py:424
  43.6 2.0 pad_maximum_fusion
  45.6 14.2 %all-to-all-done.q_ref = bf16[4,512,512]{2,1,0:T(8,128)(2,1)S(1)} async-done(((bf16[4,512,512]{2,1,0:T(8,128)(2,1)}), bf16[4,512,512]{2,1,0:T(8,128)(2,1)S(1)}, u32[]{:S(2)}, u32[]{:S(2)}) %all-to-all-start) | async-done | bytes 2097184 | tf_op jit(solution)/shard_map/all_to_all | solution.py:411
  59.8 0.0 copy-start
  59.8 1.3 copy-done
  61.1 258.7 %shard_map.55 = bf16[1,512,2048]{2,1,0:T(8,128)(2,1)} custom-call(s32[128]{0:T(128)} %reshape.61.chosen_ref, f32[4,512,128]{2,1,0:T(8,128)} %get-tuple-element.8.cos_ref, f32[4,512,128]{2,1,0:T(8,128)} %get-tuple-element.9.sin_ref, bf16[4,512,512]{2,1,0:T(8,128)(2,1)} %copy-done, bf16[4,2,512,128]{3,2,1,0:T(8,128)(2,1)} %bitcast.12, ...), custom_call_target="tpu_custom_call" | custom-call | tf_op jit(solution)/shard_map/pallas_call | solution.py:434
  319.8 3.2 copy.18
  (2 shorter events, 0.0 us)
Async XLA Ops:
  5.2 54.5 %all-to-all-start = ((bf16[4,512,512]{2,1,0:T(8,128)(2,1)}), bf16[4,512,512]{2,1,0:T(8,128)(2,1)S(1)}, u32[]{:S(2)}, u32[]{:S(2)}) async-start(bf16[4,512,512]{2,1,0:T(8,128)(2,1)} %bitcast.10), calls=%async_computation | async-start | bytes 4194304 | tf_op jit(solution)/shard_map/all_to_all | solution.py:411
  35.4 3.8 %copy-start.1 = (s32[1,4,4,8]{3,2,1,0:T(4,128)S(1)}, s32[1,4,4,8]{3,2,1,0:T(4,128)}, u32[]{:S(2)}) copy-start(s32[1,4,4,8]{3,2,1,0:T(4,128)} %param.8) | copy-start | bytes 1540
  59.8 1.3 copy-start
